TPU v7x, 32 devices: a whole 2x2x4 slice. The times are simulated.
32 devices in a mesh: wide: 8 (over y, x, core), narrow: 4 (over z).
Axes of the slice: x: 2, y: 2, z: 4, core: 2. Of those that a mesh axis runs over, the one named last changes fastest.
Arguments:
- tokens: bfloat16 [64, 208, 768], P('wide'), may hold values from -6 to 6
- grid_shape: int32 [64, 2], P('wide'), may hold values from 8 to 24, as said below
- first_gain: bfloat16 [768], replicated, may hold values from 0.5 to 1.5
- first_shift: bfloat16 [768], replicated, may hold values from -1.1953125 to 1.1953125
- qkv_weight: bfloat16 [3, 768, 768], P(None, None, 'narrow'), may hold values from -0.21875 to 0.21875
- query_bias: bfloat16 [768], P('narrow'), may hold values from -1.796875 to 1.796875
- value_bias: bfloat16 [768], P('narrow'), may hold values from -0.59765625 to 0.59765625
- rel_table: bfloat16 [12, 2212], P('narrow'), may hold values from -5 to 5
- proj_weight: bfloat16 [768, 768], P('narrow'), may hold values from -1.25 to 1.25
- proj_bias: bfloat16 [768], replicated, may hold values from -1.796875 to 1.796875
- attn_scale: bfloat16 [768], replicated, may hold values from 0.25 to 1.75
- second_gain: bfloat16 [768], replicated, may hold values from 0.5 to 1.5
- second_shift: bfloat16 [768], replicated, may hold values from -1.1953125 to 1.1953125
- up_weight: bfloat16 [768, 3072], P(None, 'narrow'), may hold values from -0.21875 to 0.21875
- up_bias: bfloat16 [3072], P('narrow'), may hold values from -3 to 3
- down_weight: bfloat16 [3072, 768], P('narrow'), may hold values from -0.15625 to 0.15625
- down_bias: bfloat16 [768], replicated, may hold values from -1.796875 to 1.796875
- mlp_scale: bfloat16 [768], replicated, may hold values from 0.25 to 1.75
- cotangent: bfloat16 [64, 208, 768], P('wide'), may hold values from -6 to 6
Outputs:
- layer_out: bfloat16 [64, 208, 768], P('wide')
- tokens_grad: float32 [64, 208, 768], P('wide')
- first_gain_grad: float32 [768], replicated
- first_shift_grad: float32 [768], replicated
- qkv_weight_grad: float32 [3, 768, 768], P(None, None, 'narrow')
- query_bias_grad: float32 [768], P('narrow')
- value_bias_grad: float32 [768], P('narrow')
- rel_table_grad: float32 [12, 2212], P('narrow')
- proj_weight_grad: float32 [768, 768], P('narrow')
- proj_bias_grad: float32 [768], replicated
- attn_scale_grad: float32 [768], replicated
- second_gain_grad: float32 [768], replicated
- second_shift_grad: float32 [768], replicated
- up_weight_grad: float32 [768, 3072], P(None, 'narrow')
- up_bias_grad: float32 [3072], P('narrow')
- down_weight_grad: float32 [3072, 768], P('narrow')
- down_bias_grad: float32 [768], replicated
- mlp_scale_grad: float32 [768], replicated
Inputs may be any that keep to these rules, and one draw needn't show every extreme that they name: `grid_shape`: each row is (height, width) of one image's patch grid, one of 14 x 14, 10 x 20, 20 x 10, 8 x 24, 24 x 8, 12 x 16, 16 x 12, 13 x 15; each of these occurs in every draw.
All inputs are finite; a program needn't handle non-finite values.
Results may differ from a plain program's by a relative error of at most 0.013.
Values sent between devices are 32-bit elements; how exact they have to be, the bound alone decides.
A program may use at most 384 MiB of HBM per device.

v0:
```python
import jax
import jax.numpy as jnp
from jax import lax
from jax.sharding import PartitionSpec as P

HD = 64
MAXG = 24
EPSILON = 1e-06
NEG_LARGE = -1000000000.0
INV_ROOT_TWO = 0.7071067811865476
INV_ROOT_TWO_PI = 0.3989422804014327


def slot_layout(grid_shape, slot_count):
    slot_ids = jnp.arange(slot_count, dtype=jnp.int32)
    patch_ids = slot_ids - 1
    grid_height = grid_shape[:, 0:1]
    grid_width = grid_shape[:, 1:2]
    is_valid = slot_ids[None, :] <= grid_height * grid_width
    row_place = jnp.floor_divide(patch_ids[None, :], grid_width)
    col_place = patch_ids[None, :] - row_place * grid_width
    span_size = 2 * MAXG - 1
    row_delta = row_place[:, :, None] - row_place[:, None, :] + (MAXG - 1)
    col_delta = col_place[:, :, None] - col_place[:, None, :] + (MAXG - 1)
    pair_index = row_delta * span_size + col_delta
    is_patch = jnp.logical_and(slot_ids[None, :] >= 1, is_valid)
    is_class = jnp.broadcast_to(slot_ids[None, :] == 0, is_patch.shape)
    both_patch = jnp.logical_and(is_patch[:, :, None], is_patch[:, None, :])
    class_query = jnp.logical_and(is_class[:, :, None], is_patch[:, None, :])
    class_key = jnp.logical_and(is_patch[:, :, None], is_class[:, None, :])
    last_entry = span_size * span_size
    pair_index = jnp.where(
        both_patch,
        pair_index,
        jnp.where(class_query, last_entry, jnp.where(class_key, last_entry + 1, last_entry + 2)),
    )
    return (pair_index, is_valid)


def norm_stats(values):
    centre = jnp.mean(values, axis=1, keepdims=True)
    centred = values - centre
    inv_root = lax.rsqrt(jnp.mean(centred * centred, axis=1, keepdims=True) + EPSILON)
    return (centred * inv_root, inv_root)


def norm_back(incoming, normed, inv_root, gain):
    scaled = incoming * gain
    return inv_root * (
        scaled
        - jnp.mean(scaled, axis=1, keepdims=True)
        - normed * jnp.mean(scaled * normed, axis=1, keepdims=True)
    )


def gelu_exact(inputs):
    return 0.5 * inputs * (1.0 + lax.erf(inputs * INV_ROOT_TWO))


def gelu_slope(inputs):
    return (
        0.5 * (1.0 + lax.erf(inputs * INV_ROOT_TWO))
        + inputs * jnp.exp(-0.5 * inputs * inputs) * INV_ROOT_TWO_PI
    )


def body(
    tokens,
    grid_shape,
    first_gain,
    first_shift,
    qkv_weight,
    query_bias,
    value_bias,
    rel_table,
    proj_weight,
    proj_bias,
    attn_scale,
    second_gain,
    second_shift,
    up_weight,
    up_bias,
    down_weight,
    down_bias,
    mlp_scale,
    cotangent,
):
    float_type = jnp.float32
    brain_type = jnp.bfloat16
    images, slot_count, model_width = tokens.shape
    local_heads, table_size = rel_table.shape
    head_size = HD
    local_width = local_heads * head_size
    total_rows = images * slot_count
    head_split = (images, slot_count, local_heads, head_size)
    query_scale = head_size ** (-0.5)
    pair_index, is_valid = slot_layout(grid_shape, slot_count)
    key_open = is_valid[:, None, None, :]
    table_f = rel_table.astype(float_type)
    table_bias = jnp.transpose(jnp.take(table_f, pair_index, axis=1), (1, 0, 2, 3))
    first_gain_f = first_gain.astype(float_type)
    second_gain_f = second_gain.astype(float_type)
    attn_scale_f = attn_scale.astype(float_type)
    mlp_scale_f = mlp_scale.astype(float_type)
    flat_in = tokens.reshape(total_rows, model_width).astype(float_type)
    normed_one, inv_one = norm_stats(flat_in)
    first_in = (normed_one * first_gain_f + first_shift.astype(float_type)).astype(brain_type)
    projected = jnp.einsum("rd,cde->cre", first_in, qkv_weight, preferred_element_type=float_type)
    queries = ((projected[0] + query_bias.astype(float_type)) * query_scale).astype(brain_type)
    keys_low = projected[1].astype(brain_type)
    values_low = (projected[2] + value_bias.astype(float_type)).astype(brain_type)
    query_heads = queries.reshape(head_split)
    key_heads = keys_low.reshape(head_split)
    value_heads = values_low.reshape(head_split)

    def attention_scores():
        raw_scores = jnp.einsum(
            "ishd,ithd->ihst", query_heads, key_heads, preferred_element_type=float_type
        )
        return jnp.where(key_open, raw_scores + table_bias, NEG_LARGE)

    scores = attention_scores()
    row_top = jnp.max(scores, axis=-1, keepdims=True)
    log_total = row_top + jnp.log(jnp.sum(jnp.exp(scores - row_top), axis=-1, keepdims=True))
    probs_low = jnp.exp(scores - log_total).astype(brain_type)
    attended = jnp.einsum(
        "ihst,ithd->ishd", probs_low, value_heads, preferred_element_type=float_type
    )
    attended = attended.reshape(total_rows, local_width).astype(brain_type)
    attn_part = jnp.dot(attended, proj_weight, preferred_element_type=float_type)
    attn_branch = lax.psum(attn_part, "narrow") + proj_bias.astype(float_type)
    middle = flat_in + attn_scale_f * attn_branch
    normed_two, inv_two = norm_stats(middle)
    second_in = (normed_two * second_gain_f + second_shift.astype(float_type)).astype(brain_type)
    up_pre = jnp.dot(second_in, up_weight, preferred_element_type=float_type) + up_bias.astype(
        float_type
    )
    hidden_low = gelu_exact(up_pre).astype(brain_type)
    down_part = jnp.dot(hidden_low, down_weight, preferred_element_type=float_type)
    mlp_branch = lax.psum(down_part, "narrow") + down_bias.astype(float_type)
    layer_out = (
        (middle + mlp_scale_f * mlp_branch)
        .astype(brain_type)
        .reshape(images, slot_count, model_width)
    )
    out_grad = cotangent.reshape(total_rows, model_width).astype(float_type) * is_valid.reshape(
        total_rows, 1
    ).astype(float_type)
    mlp_scale_grad = jnp.sum(out_grad * mlp_branch, axis=0)
    down_bias_grad = jnp.sum(out_grad, axis=0) * mlp_scale_f
    branch_low = (out_grad * mlp_scale_f).astype(brain_type)
    down_weight_grad = jnp.einsum(
        "rf,rd->fd", hidden_low, branch_low, preferred_element_type=float_type
    )
    hidden_grad = jnp.einsum(
        "rd,fd->rf", branch_low, down_weight, preferred_element_type=float_type
    )
    pre_low = (hidden_grad * gelu_slope(up_pre)).astype(brain_type)
    up_bias_grad = jnp.sum(pre_low.astype(float_type), axis=0)
    up_weight_grad = jnp.einsum("rd,rf->df", second_in, pre_low, preferred_element_type=float_type)
    second_part = jnp.einsum("rf,df->rd", pre_low, up_weight, preferred_element_type=float_type)
    second_grad = lax.psum(second_part, "narrow")
    second_gain_grad = jnp.sum(second_grad * normed_two, axis=0)
    second_shift_grad = jnp.sum(second_grad, axis=0)
    middle_grad = out_grad + norm_back(second_grad, normed_two, inv_two, second_gain_f)
    attn_scale_grad = jnp.sum(middle_grad * attn_branch, axis=0)
    proj_bias_grad = jnp.sum(middle_grad, axis=0) * attn_scale_f
    attn_low = (middle_grad * attn_scale_f).astype(brain_type)
    proj_weight_grad = jnp.einsum(
        "re,rd->ed", attended, attn_low, preferred_element_type=float_type
    )
    attended_grad = (
        jnp.einsum("rd,ed->re", attn_low, proj_weight, preferred_element_type=float_type)
        .astype(brain_type)
        .reshape(head_split)
    )
    probs_again = jnp.exp(attention_scores() - log_total)
    probs_again_low = probs_again.astype(brain_type)
    prob_grad = jnp.einsum(
        "ishd,ithd->ihst", attended_grad, value_heads, preferred_element_type=float_type
    )
    value_grad = jnp.einsum(
        "ihst,ishd->ithd", probs_again_low, attended_grad, preferred_element_type=float_type
    ).astype(brain_type)
    row_inner = jnp.sum(probs_again * prob_grad, axis=-1, keepdims=True)
    score_grad = probs_again * (prob_grad - row_inner)
    flat_index = pair_index.reshape(-1)
    head_major = jnp.transpose(score_grad, (1, 0, 2, 3)).reshape(local_heads, -1)
    rel_table_grad = jax.vmap(
        lambda entries: jax.ops.segment_sum(entries, flat_index, num_segments=table_size)
    )(head_major)
    score_low = score_grad.astype(brain_type)
    query_grad = jnp.einsum(
        "ihst,ithd->ishd", score_low, key_heads, preferred_element_type=float_type
    ).astype(brain_type) * jnp.asarray(query_scale, brain_type)
    key_grad = jnp.einsum(
        "ihst,ishd->ithd", score_low, query_heads, preferred_element_type=float_type
    ).astype(brain_type)
    query_grad = query_grad.reshape(total_rows, local_width)
    key_grad = key_grad.reshape(total_rows, local_width)
    value_grad = value_grad.reshape(total_rows, local_width)
    query_bias_grad = jnp.sum(query_grad.astype(float_type), axis=0)
    value_bias_grad = jnp.sum(value_grad.astype(float_type), axis=0)
    stacked_grads = jnp.stack([query_grad, key_grad, value_grad])
    qkv_weight_grad = jnp.einsum(
        "rd,cre->cde", first_in, stacked_grads, preferred_element_type=float_type
    )
    first_part = jnp.einsum(
        "cre,cde->rd", stacked_grads, qkv_weight, preferred_element_type=float_type
    )
    first_grad = lax.psum(first_part, "narrow")
    first_gain_grad = jnp.sum(first_grad * normed_one, axis=0)
    first_shift_grad = jnp.sum(first_grad, axis=0)
    tokens_grad = (middle_grad + norm_back(first_grad, normed_one, inv_one, first_gain_f)).reshape(
        images, slot_count, model_width
    )
    (
        first_gain_grad,
        first_shift_grad,
        qkv_weight_grad,
        query_bias_grad,
        value_bias_grad,
        rel_table_grad,
        proj_weight_grad,
        proj_bias_grad,
        attn_scale_grad,
        second_gain_grad,
        second_shift_grad,
        up_weight_grad,
        up_bias_grad,
        down_weight_grad,
        down_bias_grad,
        mlp_scale_grad,
    ) = lax.psum(
        (
            first_gain_grad,
            first_shift_grad,
            qkv_weight_grad,
            query_bias_grad,
            value_bias_grad,
            rel_table_grad,
            proj_weight_grad,
            proj_bias_grad,
            attn_scale_grad,
            second_gain_grad,
            second_shift_grad,
            up_weight_grad,
            up_bias_grad,
            down_weight_grad,
            down_bias_grad,
            mlp_scale_grad,
        ),
        "wide",
    )
    return (
        layer_out,
        tokens_grad,
        first_gain_grad,
        first_shift_grad,
        qkv_weight_grad,
        query_bias_grad,
        value_bias_grad,
        rel_table_grad,
        proj_weight_grad,
        proj_bias_grad,
        attn_scale_grad,
        second_gain_grad,
        second_shift_grad,
        up_weight_grad,
        up_bias_grad,
        down_weight_grad,
        down_bias_grad,
        mlp_scale_grad,
    )


def solution(mesh):
    return jax.shard_map(
        body,
        mesh=mesh,
        in_specs=(
            P("wide", None, None),
            P("wide", None),
            P(),
            P(),
            P(None, None, "narrow"),
            P("narrow"),
            P("narrow"),
            P("narrow", None),
            P("narrow", None),
            P(),
            P(),
            P(),
            P(),
            P(None, "narrow"),
            P("narrow"),
            P("narrow", None),
            P(),
            P(),
            P("wide", None, None),
        ),
        out_specs=(
            P("wide", None, None),
            P("wide", None, None),
            P(),
            P(),
            P(None, None, "narrow"),
            P("narrow"),
            P("narrow"),
            P("narrow", None),
            P("narrow", None),
            P(),
            P(),
            P(),
            P(),
            P(None, "narrow"),
            P("narrow"),
            P("narrow", None),
            P(),
            P(),
        ),
        check_vma=False,
    )
```

profile of v0, /device:TPU:4, one launch (start us, length us, event | category | flops | bytes accessed | tf_op | source)
XLA Modules:
  0.0 3937.0 jit_solution(91646839557959551)
XLA Ops:
  7.3 2.2 convert_reduce_fusion
  9.7 2.6 fusion.12
  14.8 2.1 compare_select_fusion
  17.1 2.5 fusion.19
  25.9 3.4 reshape.864
  29.3 2.6 broadcast_clamp_fusion
  31.9 2.4 convert_element_type.154
  34.3 3.5 squeeze.7
  37.8 3.2 squeeze.8
  41.0 1253.0 %gather_fusion = f32[346112,3]{1,0:T(8,128)} fusion(f32[3,2212]{0,1:T(8,128)S(1)} %copy.53, s32[346112]{0:T(1024)} %broadcast_clamp_fusion), kind=kCustom, calls=%fused_computation | custom fusion | bytes 9691136 | tf_op jit(solution)/shard_map/jit(_take)/gather | solution.py:100
  1294.0 102.1 %copy.55 = f32[8,208,208,3]{1,2,3,0:T(8,128)} copy(f32[8,208,208,3]{3,2,1,0:T(8,128)} %bitcast.9) | data formatting | bytes 8306688 | tf_op jit(solution)/shard_map/jit(_take)/gather | solution.py:100
  1396.1 5.7 fusion.61
  1406.9 1.9 convert_element_type.159
  1408.8 4.1 fusion.65
  1413.8 3.9 multiply_convert_fusion.2
  1417.7 181.4 %all-reduce.8.cloned.1.call-done = f32[1664,768]{1,0:T(8,128)} async-done(((f32[1664,768]{1,0:T(8,128)}), f32[1664,768]{1,0:T(8,128)}) %all-reduce.8.cloned.1.call-update) | async-done | bytes 5111824 | tf_op jit(solution)/shard_map/psum | solution.py:131
  1599.0 4.2 fusion.60
  1606.6 6.7 multiply_convert_fusion.3
  1613.3 4.7 convert_reduce_fusion.1
  1619.5 4.4 fusion.67
  1625.2 6.2 fusion.66
  1631.4 176.4 %all-reduce.10.cloned.1.call-done = f32[1664,768]{1,0:T(8,128)} async-done(((f32[1664,768]{1,0:T(8,128)}), f32[1664,768]{1,0:T(8,128)}) %all-reduce.10.cloned.1.call-update) | async-done | bytes 5111824 | tf_op jit(solution)/shard_map/psum | solution.py:162
  1807.8 5.3 multiply_reduce_fusion.2
  1814.0 6.0 multiply_reduce_fusion.3
  1819.9 2.3 copy-done.4
  1822.2 1.9 convolution_convert_fusion
  1824.1 2.6 reshape.853
  1826.7 3.7 convert_reduce_fusion.2
  1830.4 4.3 multiply_reduce_fusion.4
  1837.0 1.9 fusion.35
  1848.6 4.4 convolution_bitcast_fusion
  1853.8 2.1 select_select_fusion
  1855.9 2.6 reshape.872
  1858.6 2.5 multiply_reduce_fusion.1
  1861.2 5.7 fusion.69
  1866.9 3.8 fusion.68
  1870.9 4.1 fusion.39
  1875.1 3.0 fusion.31
  1879.1 8.8 fusion.6
  1887.9 6.2 copy.67
  1894.1 10.1 reshape.871
  1904.2 76.8 %copy.68 = f32[346112,3]{1,0:T(8,128)} copy(f32[346112,3]{0,1:T(4,128)} %bitcast.148) | data formatting | bytes 8306688 | tf_op jit(solution)/shard_map/reshape | solution.py:188
  1981.0 1865.8 %scatter_custom_fusion = f32[3,2212]{0,1:T(8,128)S(1)} fusion(s32[346112]{0:T(1024)S(1)} %reshape.872, f32[346112,3]{1,0:T(8,128)} %copy.68, f32[]{:T(128)} %constant.22.clone.1), kind=kCustom, calls=%fused_computation.92 | custom fusion | flops 1038336 | bytes 27056 | tf_op jit(solution)/shard_map/vmap()/scatter-add | solution.py:190
  3847.0 5.6 fusion.24
  3852.6 4.6 multiply_reduce_fusion
  3857.2 57.1 %all-reduce = (f32[768]{0:T(1024)}, f32[768]{0:T(1024)}, f32[192]{0:T(256)}, f32[192]{0:T(256)}, f32[3,2212]{0,1:T(8,128)S(1)}, /*index=5*/f32[768]{0:T(1024)}, ...) all-reduce(f32[768]{0:T(1024)S(1)} %get-tuple-element.56, ...), channel_id=1, replica_groups=mesh['wide'=8,'narrow'=4] {'wide'}, use_global_device_ids=true, to_apply=%region_16.17 | all-reduce | flops 13932 | bytes 111456 | tf_op jit(solution)/shard_map/psum | solution.py:234
  3915.2 7.1 fusion.23
  3922.3 2.9 copy.118
  (203 shorter events, 41.5 us)
Async XLA Ops:
  7.2 1599.4 %copy-start = (bf16[768,768]{1,0:T(8,128)(2,1)S(1)}, bf16[768,768]{1,0:T(8,128)(2,1)}, u32[]{:S(2)}) copy-start(bf16[768,768]{1,0:T(8,128)(2,1)} %param.32) | copy-start | bytes 3538948
  7.2 1591.8 %all-reduce.8.cloned.1.call-start = ((), (), s32[]{:S(2)}) async-start(), calls=%async_computation | async-start | bytes 10223616 | tf_op jit(solution)/shard_map/psum | solution.py:131
  7.3 7.5 copy-start.45
  7.3 5.0 copy-start.58
  9.5 7.3 copy-start.51
  9.6 7.3 copy-start.52
  9.7 9.9 copy-start.37
  12.9 4.0 copy-start.41
  13.2 3.7 copy-start.33
  16.9 2.7 copy-start.43
  17.0 2.6 copy-start.39
  17.0 2.6 copy-start.63
  22.4 3.2 copy-start.47
  34.3 1361.8 %copy-start.16 = (bf16[8,208,3,64]{1,0,3,2:T(8,128)(2,1)}, bf16[8,208,3,64]{1,0,3,2:T(8,128)(2,1)S(1)}, u32[]{:S(2)}) copy-start(bf16[8,208,3,64]{1,0,3,2:T(8,128)(2,1)S(1)} %convert_element_type.154) | copy-start | bytes 1916932
  1294.0 102.1 %copy-start.9 = (f32[8,208,3,64]{1,0,3,2:T(8,128)S(1)}, f32[8,208,3,64]{1,0,3,2:T(8,128)}, u32[]{:S(2)}) copy-start(f32[8,208,3,64]{1,0,3,2:T(8,128)} %squeeze.8) | copy-start | bytes 3833860
  1401.8 2.3 copy-start.3
  1401.8 2.6 copy-start.10
  1413.0 394.8 %all-reduce.10.cloned.1.call-start = ((), (), s32[]{:S(2)}) async-start(), calls=%async_computation.1 | async-start | bytes 10223616 | tf_op jit(solution)/shard_map/psum | solution.py:162
  1606.6 6.7 copy-start.14
  1606.6 6.7 copy-start.12
  1606.6 6.7 copy-start.61
  1624.0 2222.9 %all-reduce.14.cloned.1.call-start = ((), (), s32[]{:S(2)}) async-start(), calls=%async_computation.3 | async-start | bytes 20447232 | tf_op jit(solution)/shard_map/psum | solution.py:140
  1807.8 5.4 copy-start.6
  1807.8 6.2 copy-start.8
  1814.0 8.2 copy-start.29
  1819.9 2.3 copy-start.4
  1826.6 3.7 copy-start.11
  1826.7 8.1 slice-start
  1830.4 4.4 slice-start.1
  1834.7 2.3 copy-start.5
  1843.8 3.5 copy-start.25
  1844.3 2.9 copy-start.26
  1846.0 2.6 copy-start.64
  1853.1 2069.2 %all-reduce.12.cloned.1.call-start = ((), (), s32[]{:S(2)}) async-start(), calls=%async_computation.2 | async-start | bytes 14155776 | tf_op jit(solution)/shard_map/psum | solution.py:234
  1858.6 2.6 copy-start.13
  1861.2 5.7 copy-start.15
  1861.2 5.7 copy-start.22
  1870.9 4.1 copy-start.24
  1870.9 4.1 copy-start.36
  1904.2 1942.7 %copy-start.38 = (f32[1664]{0:T(1024)S(1)}, f32[1664]{0:T(1024)}, u32[]{:S(2)}) copy-start(f32[1664]{0:T(1024)} %copy-done.37) | copy-start | bytes 19972
  1904.2 1942.7 %copy-start.40 = (f32[1664]{0:T(1024)S(1)}, f32[1664]{0:T(1024)}, u32[]{:S(2)}) copy-start(f32[1664]{0:T(1024)} %copy-done.39) | copy-start | bytes 19972
  1904.2 1942.7 %copy-start.44 = (f32[768]{0:T(1024)S(1)}, f32[768]{0:T(1024)}, u32[]{:S(2)}) copy-start(f32[768]{0:T(1024)} %copy-done.43) | copy-start | bytes 9220
  3846.9 5.6 copy-start.7
  3846.9 5.6 copy-start.18
  3922.3 3.0 copy-start.30
  3922.3 3.8 copy-start.28
  3926.1 2.5 copy-start.27
  3926.1 3.9 copy-start.1
  (23 other events, 27.0 us)
Sparse Core Ops, SparseCore 0:
  1413.1 185.8 all-reduce.7
  1624.1 183.6 all-reduce.9
  1853.2 349.7 all-reduce.13
  2207.7 112.2 all-reduce.11
where the time goes:
time: 3970 us; the launch traced here: 3940 us
  other arithmetic  1930 us (49%)
  local copies, waits for them, and re-layouts  1500 us (38%)
  waiting for transfers between devices  358 us (9%)
  matrix products  68.2 us (2%)
  blocking collectives  57.1 us (1%)
    scatter-add x1, other arithmetic, body(): jax.ops.segment_sum(entries, flat_index, num_segments=table_size)  1870 us
    gather x2, local copies, waits for them, and re-layouts, body(): jnp.take(table_f, pair_index, axis=1)  1360 us
    psum x1, waiting for transfers between devices, body(): attn_branch = lax.psum(attn_part, 'narrow') + proj_bias.astype(float_type)  181 us
    psum x1, waiting for transfers between devices, body(): second_grad = lax.psum(second_part, 'narrow')  176 us
    reshape x2, local copies, waits for them, and re-layouts, body(): jnp.transpose(score_grad, (1, 0, 2, 3)).reshape(local_heads, -1)  86.9 us
  transfers between devices with their start and end apart: 4, of which 2 were waited for; matrix products, arithmetic and copies ran while one was open for 51% of the time, Pallas kernels for 0%

commit v1 on v0

--- a/solution.py
+++ b/solution.py
@@ -159,7 +159,7 @@
     up_bias_grad = jnp.sum(pre_low.astype(float_type), axis=0)
     up_weight_grad = jnp.einsum("rd,rf->df", second_in, pre_low, preferred_element_type=float_type)
     second_part = jnp.einsum("rf,df->rd", pre_low, up_weight, preferred_element_type=float_type)
-    second_grad = lax.psum(second_part, "narrow")
+    second_grad = jnp.sum(lax.all_gather(second_part, "narrow"), axis=0)
     second_gain_grad = jnp.sum(second_grad * normed_two, axis=0)
     second_shift_grad = jnp.sum(second_grad, axis=0)
     middle_grad = out_grad + norm_back(second_grad, normed_two, inv_two, second_gain_f)

time: 3970 us -> 4150 us (1.045)
  waiting for transfers between devices: 358 us -> 521 us
    all_gather x0 -> x1, waiting for transfers between devices: none -> 340 us  [body(): second_grad = jnp.sum(lax.all_gather(second_part, 'narrow'), axis=0)]
    psum x1 -> x0, waiting for transfers between devices: 176 us -> none  [body(): second_grad = lax.psum(second_part, 'narrow')]
  transfers between devices with their start and end apart: 4 -> 4, of which waited for: 2 -> 2; matrix products, arithmetic and copies ran while one was open for 51% -> 49% of each run, Pallas kernels for 0% -> 0%
where the time goes in v1:
time: 4150 us; the launch traced here: 4110 us
  other arithmetic  1950 us (47%)
  local copies, waits for them, and re-layouts  1500 us (36%)
  waiting for transfers between devices  521 us (13%)
  matrix products  68.9 us (2%)
  blocking collectives  57 us (1%)
    scatter-add x1, other arithmetic, body(): jax.ops.segment_sum(entries, flat_index, num_segments=table_size)  1870 us
    gather x2, local copies, waits for them, and re-layouts, body(): jnp.take(table_f, pair_index, axis=1)  1350 us
    all_gather x1, waiting for transfers between devices, body(): second_grad = jnp.sum(lax.all_gather(second_part, 'narrow'), axis=0)  340 us
    psum x1, waiting for transfers between devices, body(): attn_branch = lax.psum(attn_part, 'narrow') + proj_bias.astype(float_type)  181 us
    reshape x2, local copies, waits for them, and re-layouts, body(): jnp.transpose(score_grad, (1, 0, 2, 3)).reshape(local_heads, -1)  86.7 us
  transfers between devices with their start and end apart: 4, of which 2 were waited for; matrix products, arithmetic and copies ran while one was open for 49% of the time, Pallas kernels for 0%

profile of v1, /device:TPU:4, one launch (start us, length us, event | category | flops | bytes accessed | tf_op | source)
XLA Modules:
  0.0 4113.7 jit_solution(672316208479873606)
XLA Ops:
  7.3 2.2 convert_reduce_fusion
  9.7 2.6 fusion.12
  14.8 2.1 compare_select_fusion
  17.1 2.5 fusion.19
  25.8 3.4 reshape.864
  29.3 2.6 broadcast_clamp_fusion
  31.9 2.4 convert_element_type.154
  34.3 3.5 squeeze.7
  37.8 3.2 squeeze.8
  41.0 1247.6 %gather_fusion = f32[346112,3]{1,0:T(8,128)} fusion(f32[3,2212]{0,1:T(8,128)S(1)} %copy.53, s32[346112]{0:T(1024)} %broadcast_clamp_fusion), kind=kCustom, calls=%fused_computation | custom fusion | bytes 9691136 | tf_op jit(solution)/shard_map/jit(_take)/gather | solution.py:100
  1288.5 102.1 %copy.55 = f32[8,208,208,3]{1,2,3,0:T(8,128)} copy(f32[8,208,208,3]{3,2,1,0:T(8,128)} %bitcast.9) | data formatting | bytes 8306688 | tf_op jit(solution)/shard_map/jit(_take)/gather | solution.py:100
  1390.6 5.6 fusion.61
  1401.3 1.9 convert_element_type.159
  1403.3 4.2 fusion.65
  1408.3 3.8 multiply_convert_fusion.2
  1412.2 181.4 %all-reduce.7.cloned.1.call-done = f32[1664,768]{1,0:T(8,128)} async-done(((f32[1664,768]{1,0:T(8,128)}), f32[1664,768]{1,0:T(8,128)}) %all-reduce.7.cloned.1.call-update) | async-done | bytes 5111824 | tf_op jit(solution)/shard_map/psum | solution.py:131
  1593.5 4.2 fusion.60
  1601.2 6.7 multiply_convert_fusion.3
  1607.9 4.6 convert_reduce_fusion.1
  1614.1 4.5 fusion.67
  1619.9 6.6 fusion.66
  1626.5 339.6 %all-gather.3.cloned.1.call-done = f32[6656,768]{1,0:T(8,128)} async-done(((f32[1664,768]{1,0:T(8,128)}), f32[6656,768]{1,0:T(8,128)}) %all-gather.3.cloned.1.call-update) | async-done | bytes 20447248 | tf_op jit(solution)/shard_map/all_gather | solution.py:162
  1966.0 10.4 reduce_sum.207
  1976.4 6.0 multiply_reduce_fusion.2
  1982.7 5.9 multiply_reduce_fusion.3
  1988.6 2.3 copy-done.4
  1992.8 2.6 reshape.853
  1995.4 3.7 convert_reduce_fusion.2
  1999.1 4.3 multiply_reduce_fusion.4
  2017.4 4.6 convolution_bitcast_fusion
  2022.7 2.1 select_select_fusion
  2024.9 2.6 reshape.872
  2027.5 2.5 multiply_reduce_fusion.1
  2030.1 5.7 fusion.69
  2035.7 3.8 fusion.68
  2039.8 4.1 fusion.39
  2043.9 3.0 fusion.31
  2047.9 8.8 fusion.6
  2056.7 6.2 copy.67
  2062.9 10.0 reshape.871
  2072.9 76.8 %copy.68 = f32[346112,3]{1,0:T(8,128)} copy(f32[346112,3]{0,1:T(4,128)} %bitcast.150) | data formatting | bytes 8306688 | tf_op jit(solution)/shard_map/reshape | solution.py:188
  2149.6 1865.8 %scatter_custom_fusion = f32[3,2212]{0,1:T(8,128)S(1)} fusion(s32[346112]{0:T(1024)S(1)} %reshape.872, f32[346112,3]{1,0:T(8,128)} %copy.68, f32[]{:T(128)} %constant.22.clone.1), kind=kCustom, calls=%fused_computation.92 | custom fusion | flops 1038336 | bytes 27056 | tf_op jit(solution)/shard_map/vmap()/scatter-add | solution.py:190
  4015.5 7.9 reduce_sum.222
  4023.5 5.6 fusion.24
  4029.1 5.1 multiply_reduce_fusion
  4034.2 57.0 %all-reduce = (f32[768]{0:T(1024)}, f32[768]{0:T(1024)}, f32[192]{0:T(256)}, f32[192]{0:T(256)}, f32[3,2212]{0,1:T(8,128)S(1)}, /*index=5*/f32[768]{0:T(1024)}, ...) all-reduce(f32[768]{0:T(1024)S(1)} %get-tuple-element.56, ...), channel_id=1, replica_groups=mesh['wide'=8,'narrow'=4] {'wide'}, use_global_device_ids=true, to_apply=%region_16.17 | all-reduce | flops 13932 | bytes 111456 | tf_op jit(solution)/shard_map/psum | solution.py:234
  4092.2 7.1 fusion.23
  4099.3 2.9 copy.117
  (211 shorter events, 44.7 us)
Async XLA Ops:
  7.2 1594.0 %copy-start = (bf16[768,768]{1,0:T(8,128)(2,1)S(1)}, bf16[768,768]{1,0:T(8,128)(2,1)}, u32[]{:S(2)}) copy-start(bf16[768,768]{1,0:T(8,128)(2,1)} %param.32) | copy-start | bytes 3538948
  7.2 1586.3 %all-reduce.7.cloned.1.call-start = ((), (), s32[]{:S(2)}) async-start(), calls=%async_computation | async-start | bytes 10223616 | tf_op jit(solution)/shard_map/psum | solution.py:131
  7.3 7.5 copy-start.47
  7.3 5.0 copy-start.61
  9.5 7.3 copy-start.54
  9.6 7.3 copy-start.55
  9.7 9.9 copy-start.37
  12.9 4.0 copy-start.41
  13.2 3.7 copy-start.33
  16.9 2.7 copy-start.43
  17.0 2.6 copy-start.39
  17.0 2.6 copy-start.66
  22.4 3.2 copy-start.49
  34.3 1356.3 %copy-start.16 = (bf16[8,208,3,64]{1,0,3,2:T(8,128)(2,1)}, bf16[8,208,3,64]{1,0,3,2:T(8,128)(2,1)S(1)}, u32[]{:S(2)}) copy-start(bf16[8,208,3,64]{1,0,3,2:T(8,128)(2,1)S(1)} %convert_element_type.154) | copy-start | bytes 1916932
  1288.5 102.1 %copy-start.9 = (f32[8,208,3,64]{1,0,3,2:T(8,128)S(1)}, f32[8,208,3,64]{1,0,3,2:T(8,128)}, u32[]{:S(2)}) copy-start(f32[8,208,3,64]{1,0,3,2:T(8,128)} %squeeze.8) | copy-start | bytes 3833860
  1396.2 2.6 copy-start.10
  1407.5 558.5 %all-gather.3.cloned.1.call-start = ((), (), s32[]{:S(2)}) async-start(), calls=%async_computation.1 | async-start | bytes 25559040 | tf_op jit(solution)/shard_map/all_gather | solution.py:162
  1408.2 3.9 copy-start.45
  1601.2 6.7 copy-start.14
  1601.2 6.7 copy-start.12
  1601.2 6.7 copy-start.64
  1618.6 2404.8 %all-reduce.11.cloned.1.call-start = ((), (), s32[]{:S(2)}) async-start(), calls=%async_computation.3 | async-start | bytes 20447232 | tf_op jit(solution)/shard_map/psum | solution.py:140
  1976.4 6.0 copy-start.6
  1976.4 6.2 copy-start.7
  1982.7 8.3 copy-start.29
  1995.4 3.7 copy-start.11
  1995.4 8.1 slice-start
  1999.1 4.4 slice-start.1
  2012.5 3.5 copy-start.25
  2013.0 2.9 copy-start.26
  2014.7 2.7 copy-start.67
  2022.0 2077.2 %all-reduce.9.cloned.1.call-start = ((), (), s32[]{:S(2)}) async-start(), calls=%async_computation.2 | async-start | bytes 14155776 | tf_op jit(solution)/shard_map/psum | solution.py:234
  2027.5 2.5 copy-start.13
  2030.1 5.7 copy-start.15
  2030.1 5.7 copy-start.22
  2039.8 4.1 copy-start.24
  2039.8 4.1 copy-start.36
  4015.5 7.9 copy-start.53
  4015.5 8.0 copy-start.38
  4015.5 8.0 copy-start.40
  4015.5 8.0 copy-start.44
  4023.5 5.6 copy-start.8
  4023.5 5.6 copy-start.18
  4023.5 5.6 copy-start.46
  4099.3 3.0 copy-start.30
  4099.3 3.8 copy-start.28
  4103.1 2.5 copy-start.27
  4103.1 3.9 copy-start.1
  (26 other events, 33.9 us)
Sparse Core Ops, SparseCore 0:
  1407.6 185.8 all-reduce.6
  1618.7 347.2 all-gather.2
  2022.2 349.3 all-reduce.10
  2376.3 112.2 all-reduce.8
